TPU v7x, 32 devices: a whole 2x2x4 slice. The times are simulated.
32 devices in a mesh: row: 8 (over y, x, core), col: 4 (over z).
Axes of the slice: x: 2, y: 2, z: 4, core: 2. Of those that a mesh axis runs over, the one named last changes fastest.
Arguments:
- homolog_embedding: bfloat16 [32, 1024, 64], P(('row', 'col')), may hold values from -6 to 6
- split_mapping_matrix: bfloat16 [64, 64], replicated, may hold values from -0.75 to 0.75
- couple_mapping_matrix: bfloat16 [1024, 128], replicated, may hold values from -1.5 to 1.5
- couple_offset_vector: bfloat16 [128], replicated, may hold values from -3 to 3
- incoming_adjoint_couple: bfloat16 [1024, 1024, 128], P('row', 'col'), may hold values from -0.29882812 to 0.29882812
Outputs:
- pair_delta_output: bfloat16 [1024, 1024, 128], P('row', 'col')
- alignment_gradient: bfloat16 [32, 1024, 64], P(('row', 'col'))
- out_weight_grad: float32 [1024, 128], replicated
All inputs are finite; a program needn't handle non-finite values.
Results may differ from a plain program's by a relative error of at most 0.015.
Values may be sent and summed in bfloat16 or wider, within the bound.
No kernel may reach another device: no remote copies, remote signals or barrier semaphores. Data moves between devices by JAX's collectives and lax.ppermute only.
A program may use at most 128 MiB of HBM per device.

v0:
```python
import math

import jax
import jax.numpy as jnp
from jax import lax
from jax.sharding import PartitionSpec as P


def standardize_features(homolog_embedding):
    mapped_halves = homolog_embedding.astype(jnp.float32)
    center = jnp.mean(mapped_halves, axis=-1, keepdims=True)
    spread = jnp.mean((mapped_halves - center) * (mapped_halves - center), axis=-1, keepdims=True)
    reciprocal_spread = lax.rsqrt(spread + 1e-05)
    return ((mapped_halves - center) * reciprocal_spread, reciprocal_spread)


def regroup(mapped_halves, outer_count, inner_count):
    shaped = mapped_halves.reshape((outer_count, inner_count, -1) + mapped_halves.shape[1:])
    return jnp.swapaxes(shaped, 0, 1).reshape(mapped_halves.shape)


def on_device(
    homolog_embedding,
    split_mapping_matrix,
    couple_mapping_matrix,
    couple_offset_vector,
    incoming_adjoint_couple,
):
    rows_count = lax.axis_size("row")
    cols_count = lax.axis_size("col")
    width = split_mapping_matrix.shape[1] // 2
    standardized_activations, reciprocal_spread = standardize_features(homolog_embedding)
    normalized_input = standardized_activations.astype(jnp.bfloat16)
    factors = jnp.dot(
        normalized_input, split_mapping_matrix, preferred_element_type=jnp.float32
    ).astype(jnp.bfloat16)
    left = factors[..., :width]
    right = factors[..., width:]
    left_all = lax.all_gather(left, "col", axis=0, tiled=True)
    left_panel = lax.all_to_all(left_all, "row", split_axis=1, concat_axis=0, tiled=True)
    right_all = lax.all_gather(right, "row", axis=0, tiled=True)
    right_panel = regroup(
        lax.all_to_all(right_all, "col", split_axis=1, concat_axis=0, tiled=True),
        cols_count,
        rows_count,
    )
    seq_total = left_panel.shape[0]
    rows_local = left_panel.shape[1]
    cols_local = right_panel.shape[1]
    channels = incoming_adjoint_couple.shape[2]
    step_rows = math.gcd(rows_local, 16)
    count = rows_local // step_rows
    left_blocks = left_panel.reshape(seq_total, count, step_rows, width).transpose(1, 0, 2, 3)
    cot_blocks = incoming_adjoint_couple.reshape(count, step_rows, cols_local, channels)
    bias_wide = couple_offset_vector.astype(jnp.float32)
    weight_back = couple_mapping_matrix.T

    def advance(carry, inputs):
        weight_sum, right_sum = carry
        left_block, cot_block = inputs
        outer = (
            jnp.einsum("sic,sje->ijce", left_block, right_panel, preferred_element_type=jnp.float32)
            / seq_total
        )
        flat = outer.astype(jnp.bfloat16).reshape(step_rows * cols_local, width * width)
        update = (
            jnp.dot(flat, couple_mapping_matrix, preferred_element_type=jnp.float32) + bias_wide
        ).astype(jnp.bfloat16)
        grad_rows = cot_block.reshape(step_rows * cols_local, channels)
        outer_grad = jnp.dot(grad_rows, weight_back, preferred_element_type=jnp.float32).astype(
            jnp.bfloat16
        )
        outer_grad = outer_grad.reshape(step_rows, cols_local, width, width)
        weight_sum = weight_sum + lax.dot_general(
            flat, grad_rows, (((0,), (0,)), ((), ())), preferred_element_type=jnp.float32
        )
        left_grad = (
            jnp.einsum("ijce,sje->sic", outer_grad, right_panel, preferred_element_type=jnp.float32)
            / seq_total
        )
        right_sum = (
            right_sum
            + jnp.einsum(
                "ijce,sic->sje", outer_grad, left_block, preferred_element_type=jnp.float32
            )
            / seq_total
        )
        return (
            (weight_sum, right_sum),
            (update.reshape(step_rows, cols_local, channels), left_grad),
        )

    start = (
        jnp.zeros((width * width, channels), jnp.float32),
        jnp.zeros((seq_total, cols_local, width), jnp.float32),
    )
    (weight_part, right_grad), (updates, left_grads) = lax.scan(
        advance, start, (left_blocks, cot_blocks)
    )
    pair_delta_output = updates.reshape(rows_local, cols_local, channels)
    left_grad = left_grads.transpose(1, 0, 2, 3).reshape(seq_total, rows_local, width)
    left_home = lax.all_to_all(
        left_grad.astype(jnp.bfloat16), "row", split_axis=0, concat_axis=1, tiled=True
    ).astype(left_grad.dtype)
    left_back = lax.psum_scatter(
        left_home.astype(jnp.bfloat16), "col", scatter_dimension=0, tiled=True
    )
    right_home = lax.all_to_all(
        regroup(right_grad, rows_count, cols_count).astype(jnp.bfloat16),
        "col",
        split_axis=0,
        concat_axis=1,
        tiled=True,
    )
    right_back = lax.psum_scatter(right_home, "row", scatter_dimension=0, tiled=True)
    factor_weight_gradient = lax.psum(weight_part, ("row", "col"))
    both = jnp.concatenate([left_back, right_back], axis=-1)
    normalized_gradient = jnp.dot(both, split_mapping_matrix.T, preferred_element_type=jnp.float32)
    first_factor = jnp.mean(normalized_gradient, axis=-1, keepdims=True)
    second_factor = jnp.mean(normalized_gradient * standardized_activations, axis=-1, keepdims=True)
    alignment_gradient = (
        reciprocal_spread
        * (normalized_gradient - first_factor - standardized_activations * second_factor)
    ).astype(jnp.bfloat16)
    return (pair_delta_output, alignment_gradient, factor_weight_gradient)


def solution(mesh):
    placed = (P(("row", "col"), None, None), P(), P(), P(), P("row", "col", None))
    return jax.shard_map(
        on_device,
        mesh=mesh,
        in_specs=placed,
        out_specs=(P("row", "col", None), P(("row", "col"), None, None), P()),
        check_vma=False,
    )
```

profile of v0, /device:TPU:1, one launch (start us, length us, event | category | flops | bytes accessed | tf_op | source)
XLA Modules:
  0.0 929.2 jit_solution(15135859743567451930)
XLA Ops:
  11.2 13.3 %all_gather.6 = bf16[4,1024,32]{1,2,0:T(8,128)(2,1)S(1)} all-gather(bf16[1,1024,32]{1,2,0:T(8,128)(2,1)S(1)} %get-tuple-element.172), channel_id=1, replica_groups=mesh['row'=8,'col'=4] {'col'}, dimensions={0}, use_global_device_ids=true | all-gather | bytes 327680 | tf_op jit(solution)/shard_map/all_gather | solution.py:39
  56.0 11.7 %all-to-all-done.1 = bf16[4,2,32768]{2,1,0:T(2,128)(2,1)S(1)} async-done(((bf16[4,2,32768]{2,1,0:T(2,128)(2,1)}), bf16[4,2,32768]{2,1,0:T(2,128)(2,1)S(1)}, u32[]{:S(2)}, u32[]{:S(2)}) %all-to-all-start.1) | async-done | bytes 524320 | tf_op jit(solution)/shard_map/all_to_all | solution.py:43
  73.5 679.0 %while.17 = (s32[]{:T(128)}, f32[1024,128]{1,0:T(8,128)S(1)}, f32[32,256,32]{1,0,2:T(8,128)S(1)}, bf16[8,16,256,128]{3,2,1,0:T(8,128)(2,1)}, bf16[8,32,16,32]{1,...) while((s32[]{:T(128)}, f32[1024,128]{1,0:T(8,128)S(1)}, ...), condition=%wide.region_3.4_spmd.clone, body=%wide.region_2.3_spmd.clone.sunk | while | flops 4041228288 | bytes 164564688 | solution.py:97
  111.7 12.3 %copy.105 = bf16[128,8,16,256]{3,1,2,0:T(8,128)(2,1)} copy(bf16[128,8,16,256]{3,2,1,0:T(8,128)(2,1)} %bitcast.161) | data formatting | bytes 16777216 | tf_op jit(solution)/shard_map/while
  143.6 11.4 %copy.106 = bf16[4096,1024]{0,1:T(8,128)(2,1)} copy(bf16[4096,1024]{1,0:T(8,128)(2,1)} %convolution_convert_fusion.3) | data formatting | bytes 16777216 | tf_op jit(solution)/shard_map/while/body/eval_jaxpr/convert_element_type | solution.py:70
  182.7 11.4 %copy.104 = bf16[16,256,32,32]{1,0,3,2:T(8,128)(2,1)} copy(bf16[16,256,32,32]{1,2,3,0:T(8,128)(2,1)} %fusion.77) | data formatting | bytes 16777216 | tf_op jit(solution)/shard_map/while/body/eval_jaxpr/convert_element_type | solution.py:65
  194.1 12.3 %copy.105 = bf16[128,8,16,256]{3,1,2,0:T(8,128)(2,1)} copy(bf16[128,8,16,256]{3,2,1,0:T(8,128)(2,1)} %bitcast.161) | data formatting | bytes 16777216 | tf_op jit(solution)/shard_map/while
  225.9 11.4 %copy.106 = bf16[4096,1024]{0,1:T(8,128)(2,1)} copy(bf16[4096,1024]{1,0:T(8,128)(2,1)} %convolution_convert_fusion.3) | data formatting | bytes 16777216 | tf_op jit(solution)/shard_map/while/body/eval_jaxpr/convert_element_type | solution.py:70
  276.4 12.3 %copy.105 = bf16[128,8,16,256]{3,1,2,0:T(8,128)(2,1)} copy(bf16[128,8,16,256]{3,2,1,0:T(8,128)(2,1)} %bitcast.161) | data formatting | bytes 16777216 | tf_op jit(solution)/shard_map/while
  308.2 11.4 %copy.106 = bf16[4096,1024]{0,1:T(8,128)(2,1)} copy(bf16[4096,1024]{1,0:T(8,128)(2,1)} %convolution_convert_fusion.3) | data formatting | bytes 16777216 | tf_op jit(solution)/shard_map/while/body/eval_jaxpr/convert_element_type | solution.py:70
  358.7 12.3 %copy.105 = bf16[128,8,16,256]{3,1,2,0:T(8,128)(2,1)} copy(bf16[128,8,16,256]{3,2,1,0:T(8,128)(2,1)} %bitcast.161) | data formatting | bytes 16777216 | tf_op jit(solution)/shard_map/while
  390.5 11.4 %copy.106 = bf16[4096,1024]{0,1:T(8,128)(2,1)} copy(bf16[4096,1024]{1,0:T(8,128)(2,1)} %convolution_convert_fusion.3) | data formatting | bytes 16777216 | tf_op jit(solution)/shard_map/while/body/eval_jaxpr/convert_element_type | solution.py:70
  441.0 12.3 %copy.105 = bf16[128,8,16,256]{3,1,2,0:T(8,128)(2,1)} copy(bf16[128,8,16,256]{3,2,1,0:T(8,128)(2,1)} %bitcast.161) | data formatting | bytes 16777216 | tf_op jit(solution)/shard_map/while
  472.8 11.4 %copy.106 = bf16[4096,1024]{0,1:T(8,128)(2,1)} copy(bf16[4096,1024]{1,0:T(8,128)(2,1)} %convolution_convert_fusion.3) | data formatting | bytes 16777216 | tf_op jit(solution)/shard_map/while/body/eval_jaxpr/convert_element_type | solution.py:70
  511.9 11.4 %copy.104 = bf16[16,256,32,32]{1,0,3,2:T(8,128)(2,1)} copy(bf16[16,256,32,32]{1,2,3,0:T(8,128)(2,1)} %fusion.77) | data formatting | bytes 16777216 | tf_op jit(solution)/shard_map/while/body/eval_jaxpr/convert_element_type | solution.py:65
  523.3 12.3 %copy.105 = bf16[128,8,16,256]{3,1,2,0:T(8,128)(2,1)} copy(bf16[128,8,16,256]{3,2,1,0:T(8,128)(2,1)} %bitcast.161) | data formatting | bytes 16777216 | tf_op jit(solution)/shard_map/while
  555.1 11.4 %copy.106 = bf16[4096,1024]{0,1:T(8,128)(2,1)} copy(bf16[4096,1024]{1,0:T(8,128)(2,1)} %convolution_convert_fusion.3) | data formatting | bytes 16777216 | tf_op jit(solution)/shard_map/while/body/eval_jaxpr/convert_element_type | solution.py:70
  605.7 12.3 %copy.105 = bf16[128,8,16,256]{3,1,2,0:T(8,128)(2,1)} copy(bf16[128,8,16,256]{3,2,1,0:T(8,128)(2,1)} %bitcast.161) | data formatting | bytes 16777216 | tf_op jit(solution)/shard_map/while
  637.5 11.4 %copy.106 = bf16[4096,1024]{0,1:T(8,128)(2,1)} copy(bf16[4096,1024]{1,0:T(8,128)(2,1)} %convolution_convert_fusion.3) | data formatting | bytes 16777216 | tf_op jit(solution)/shard_map/while/body/eval_jaxpr/convert_element_type | solution.py:70
  688.0 12.3 %copy.105 = bf16[128,8,16,256]{3,1,2,0:T(8,128)(2,1)} copy(bf16[128,8,16,256]{3,2,1,0:T(8,128)(2,1)} %bitcast.161) | data formatting | bytes 16777216 | tf_op jit(solution)/shard_map/while
  719.8 11.4 %copy.106 = bf16[4096,1024]{0,1:T(8,128)(2,1)} copy(bf16[4096,1024]{1,0:T(8,128)(2,1)} %convolution_convert_fusion.3) | data formatting | bytes 16777216 | tf_op jit(solution)/shard_map/while/body/eval_jaxpr/convert_element_type | solution.py:70
  771.6 14.8 %all-to-all-done.3 = bf16[32,256,32]{1,2,0:T(8,128)(2,1)S(1)} async-done(((bf16[32,256,32]{1,2,0:T(8,128)(2,1)}), bf16[32,256,32]{1,2,0:T(8,128)(2,1)S(1)}, u32[]{:S(2)}, u32[]{:S(2)}) %all-to-all-start.3) | async-done | bytes 524320 | tf_op jit(solution)/shard_map/all_to_all | solution.py:108
  791.5 39.1 %reduce-scatter.5.cloned.1.call-done = bf16[1,1024,32]{1,2,0:T(8,128)(2,1)} async-done(((bf16[8,1024,32]{1,2,0:T(8,128)(2,1)}), bf16[1,1024,32]{1,2,0:T(8,128)(2,1)}) %reduce-scatter.5.cloned.1.call-update) | async-done | bytes 65552 | tf_op jit(solution)/shard_map/reduce_scatter | solution.py:115
  832.5 87.1 %all-reduce.2.cloned.1.call-done = f32[1024,128]{1,0:T(8,128)} async-done(((f32[1024,128]{1,0:T(8,128)}), f32[1024,128]{1,0:T(8,128)}) %all-reduce.2.cloned.1.call-update) | async-done | bytes 524304 | tf_op jit(solution)/shard_map/psum | solution.py:116
  (200 shorter events, 514.3 us)
Async XLA Ops:
  8.0 45.5 %copy-start.5 = (bf16[1024,128]{1,0:T(8,128)(2,1)S(1)}, bf16[1024,128]{1,0:T(8,128)(2,1)}, u32[]{:S(2)}) copy-start(bf16[1024,128]{1,0:T(8,128)(2,1)} %param.9) | copy-start | bytes 786436
  24.5 29.2 %copy-start.11 = (bf16[128]{0:T(256)(128)(2,1)S(1)}, bf16[128]{0:T(256)(128)(2,1)}, u32[]{:S(2)}) copy-start(bf16[128]{0:T(256)(128)(2,1)} %param.10) | copy-start | bytes 772
  26.9 21.8 %all-to-all-start = ((bf16[8,2,8192]{2,1,0:T(2,128)(2,1)}), bf16[8,2,8192]{2,1,0:T(2,128)(2,1)S(1)}, u32[]{:S(2)}, u32[]{:S(2)}) async-start(bf16[8,2,8192]{2,1,0:T(2,128)(2,1)} %reshape.107), calls=%async_computation | async-start | bytes 524288 | tf_op jit(solution)/shard_map/all_to_all | solution.py:40
  48.6 19.0 %all-to-all-start.1 = ((bf16[4,2,32768]{2,1,0:T(2,128)(2,1)}), bf16[4,2,32768]{2,1,0:T(2,128)(2,1)S(1)}, u32[]{:S(2)}, u32[]{:S(2)}) async-start(bf16[4,2,32768]{2,1,0:T(2,128)(2,1)} %reshape.109), calls=%async_computation.1 | async-start | bytes 1048576 | tf_op jit(solution)/shard_map/all_to_all | solution.py:43
  54.7 18.7 %copy-start.3 = (f32[1024,128]{1,0:T(8,128)S(1)}, f32[1024,128]{1,0:T(8,128)}, u32[]{:S(2)}) copy-start(f32[1024,128]{1,0:T(8,128)} %custom-call) | copy-start | bytes 1572868
  111.7 12.3 %copy-start.12 = (f32[128]{0:T(128)S(1)}, f32[128]{0:T(128)}, u32[]{:S(2)}) copy-start(f32[128]{0:T(128)} %get-tuple-element.284) | copy-start | bytes 1540 | tf_op jit(solution)/shard_map/while
  194.1 12.3 %copy-start.6 = (bf16[1024,128]{1,0:T(8,128)(2,1)S(1)}, bf16[1024,128]{1,0:T(8,128)(2,1)}, u32[]{:S(2)}) copy-start(bf16[1024,128]{1,0:T(8,128)(2,1)} %get-tuple-element.283) | copy-start | bytes 786436 | tf_op jit(solution)/shard_map/while
  194.1 12.3 %copy-start.12 = (f32[128]{0:T(128)S(1)}, f32[128]{0:T(128)}, u32[]{:S(2)}) copy-start(f32[128]{0:T(128)} %get-tuple-element.284) | copy-start | bytes 1540 | tf_op jit(solution)/shard_map/while
  276.4 12.3 %copy-start.6 = (bf16[1024,128]{1,0:T(8,128)(2,1)S(1)}, bf16[1024,128]{1,0:T(8,128)(2,1)}, u32[]{:S(2)}) copy-start(bf16[1024,128]{1,0:T(8,128)(2,1)} %get-tuple-element.283) | copy-start | bytes 786436 | tf_op jit(solution)/shard_map/while
  276.4 12.3 %copy-start.12 = (f32[128]{0:T(128)S(1)}, f32[128]{0:T(128)}, u32[]{:S(2)}) copy-start(f32[128]{0:T(128)} %get-tuple-element.284) | copy-start | bytes 1540 | tf_op jit(solution)/shard_map/while
  358.7 12.3 %copy-start.12 = (f32[128]{0:T(128)S(1)}, f32[128]{0:T(128)}, u32[]{:S(2)}) copy-start(f32[128]{0:T(128)} %get-tuple-element.284) | copy-start | bytes 1540 | tf_op jit(solution)/shard_map/while
  441.0 12.3 %copy-start.12 = (f32[128]{0:T(128)S(1)}, f32[128]{0:T(128)}, u32[]{:S(2)}) copy-start(f32[128]{0:T(128)} %get-tuple-element.284) | copy-start | bytes 1540 | tf_op jit(solution)/shard_map/while
  523.3 12.3 %copy-start.12 = (f32[128]{0:T(128)S(1)}, f32[128]{0:T(128)}, u32[]{:S(2)}) copy-start(f32[128]{0:T(128)} %get-tuple-element.284) | copy-start | bytes 1540 | tf_op jit(solution)/shard_map/while
  605.7 12.3 %copy-start.12 = (f32[128]{0:T(128)S(1)}, f32[128]{0:T(128)}, u32[]{:S(2)}) copy-start(f32[128]{0:T(128)} %get-tuple-element.284) | copy-start | bytes 1540 | tf_op jit(solution)/shard_map/while
  688.0 12.3 %copy-start.12 = (f32[128]{0:T(128)S(1)}, f32[128]{0:T(128)}, u32[]{:S(2)}) copy-start(f32[128]{0:T(128)} %get-tuple-element.284) | copy-start | bytes 1540 | tf_op jit(solution)/shard_map/while
  752.5 34.8 %copy-start.4 = (f32[1024,128]{1,0:T(8,128)}, f32[1024,128]{1,0:T(8,128)S(1)}, u32[]{:S(2)}) copy-start(f32[1024,128]{1,0:T(8,128)S(1)} %get-tuple-element.66) | copy-start | bytes 1572868
  752.5 78.2 %copy-start.2 = (bf16[1,1024,64]{1,2,0:T(8,128)(2,1)S(1)}, bf16[1,1024,64]{1,2,0:T(8,128)(2,1)}, u32[]{:S(2)}) copy-start(bf16[1,1024,64]{1,2,0:T(8,128)(2,1)} %param.7) | copy-start | bytes 393220
  752.5 78.2 %copy-start.8 = (f32[1024]{0:T(1024)S(1)}, f32[1024]{0:T(1024)}, u32[]{:S(2)}) copy-start(f32[1024]{0:T(1024)} %copy-done.7) | copy-start | bytes 12292
  752.5 78.1 %copy-start.10 = (f32[1024]{0:T(1024)S(1)}, f32[1024]{0:T(1024)}, u32[]{:S(2)}) copy-start(f32[1024]{0:T(1024)} %copy-done.9) | copy-start | bytes 12292
  756.9 10.3 %all-to-all-start.2 = ((bf16[32,128,32]{1,2,0:T(8,128)(2,1)}), bf16[32,128,32]{1,2,0:T(8,128)(2,1)S(1)}, u32[]{:S(2)}, u32[]{:S(2)}) async-start(bf16[32,128,32]{1,2,0:T(8,128)(2,1)} %copy.67), calls=%async_computation.2 | async-start | bytes 524288 | tf_op jit(solution)/shard_map/all_to_all | solution.py:102
  767.2 19.1 %all-to-all-start.3 = ((bf16[32,256,32]{1,2,0:T(8,128)(2,1)}), bf16[32,256,32]{1,2,0:T(8,128)(2,1)S(1)}, u32[]{:S(2)}, u32[]{:S(2)}) async-start(bf16[32,256,32]{1,2,0:T(8,128)(2,1)} %bitcast.20), calls=%async_computation.4 | async-start | bytes 1048576 | tf_op jit(solution)/shard_map/all_to_all | solution.py:108
  770.7 20.8 %reduce-scatter.3.cloned.1.call-start = ((), (), s32[]{:S(2)}) async-start(), calls=%async_computation.6 | async-start | bytes 327680 | tf_op jit(solution)/shard_map/reduce_scatter | solution.py:105
  771.6 59.1 %reduce-scatter.5.cloned.1.call-start = ((), (), s32[]{:S(2)}) async-start(), calls=%async_computation.7 | async-start | bytes 589824 | tf_op jit(solution)/shard_map/reduce_scatter | solution.py:115
  787.2 132.3 %all-reduce.2.cloned.1.call-start = ((), (), s32[]{:S(2)}) async-start(), calls=%async_computation.8 | async-start | bytes 1048576 | tf_op jit(solution)/shard_map/psum | solution.py:116
  (17 other events, 146.2 us)
Sparse Core Ops, SparseCore 0:
  773.8 17.7 reduce-scatter.2
  795.2 35.4 reduce-scatter.4
Sparse Core Ops, SparseCore 1:
  793.0 126.5 all-reduce.1
where the time goes:
time: 940 us; the launch traced here: 929 us
  local copies, waits for them, and re-layouts  410 us (44%)
  matrix products  274 us (29%)
  waiting for transfers between devices  161 us (17%)
  blocking collectives  24.4 us (3%)
  loops' own time  20.7 us (2%)
  starting transfers between devices  19.2 us (2%)
  between operations  16.1 us (2%)
    while x64, local copies, waits for them, and re-layouts  176 us
    convert_element_type x8, local copies, waits for them, and re-layouts, advance(): jnp.dot(grad_rows, weight_back, preferred_element_type=jnp.float32)  91.1 us
    convert_element_type x8, local copies, waits for them, and re-layouts, advance(): outer.astype(jnp.bfloat16).reshape(step_rows * cols_local, width * width)  91 us
    psum x1, waiting for transfers between devices, on_device(): factor_weight_gradient = lax.psum(weight_part, ('row', 'col'))  87.1 us
    dot_general x8, matrix products, advance(): jnp.einsum('ijce,sic->sje', outer_grad, left_block, preferred_element_typ...  67 us
    dot_general x8, matrix products, advance(): lax.dot_general(flat, grad_rows, (((0,), (0,)), ((), ())), preferred_elem...  46.3 us
    dot_general x8, matrix products, advance(): jnp.dot(flat, couple_mapping_matrix, preferred_element_type=jnp.float32)  46.1 us
    dot_general x8, matrix products, advance(): jnp.dot(grad_rows, weight_back, preferred_element_type=jnp.float32)  44.5 us
  transfers between devices with their start and end apart: 7, of which 6 were waited for; matrix products, arithmetic and copies ran while one was open for 1% of the time, Pallas kernels for 0%

commit v1 on v0

v1 whole, which is shorter than its diff:
```python
import functools
import math

import jax
import jax.numpy as jnp
from jax import lax
from jax.experimental import pallas as pl
from jax.experimental.pallas import tpu as pltpu
from jax.sharding import PartitionSpec as P

F32 = jnp.float32
BF16 = jnp.bfloat16
AXES = ("row", "col")
LANES = 128
VMEM_BYTES = 56 << 20
DEPTH = 4
STORED_BYTES = 1 << 25


def dot(a, b, da=1, db=0):
    return lax.dot_general(a, b, (((da,), (db,)), ((), ())), preferred_element_type=F32)


def whole(shape):
    return pl.BlockSpec(shape, lambda *_: (0,) * len(shape))


def call(kernel, grid, ins, outs, scratch, flops, args, aliases={}):
    nbytes = sum(a.size * a.dtype.itemsize for a in args)
    nbytes += sum(math.prod(o.shape) * o.dtype.itemsize for _, o in outs)
    return pl.pallas_call(
        kernel,
        grid_spec=pltpu.PrefetchScalarGridSpec(
            num_scalar_prefetch=0,
            grid=grid,
            in_specs=ins,
            out_specs=[s for s, _ in outs],
            scratch_shapes=scratch,
        ),
        out_shape=[o for _, o in outs],
        input_output_aliases=aliases,
        compiler_params=pltpu.CompilerParams(vmem_limit_bytes=VMEM_BYTES),
        cost_estimate=pl.CostEstimate(flops=flops, bytes_accessed=nbytes, transcendentals=0),
    )(*args)


def normalize(x):
    mu = jnp.mean(x, axis=0, keepdims=True)
    var = jnp.mean((x - mu) * (x - mu), axis=0, keepdims=True)
    rstd = lax.rsqrt(var + 1e-05)
    return (x - mu) * rstd, rstd


def project_kernel(rows, cols, x_ref, w_ref, left_ref, right_ref):
    xhat, _ = normalize(x_ref[0].astype(F32))
    width = w_ref.shape[1] // 2
    part, per_col = left_ref.shape[1], right_ref.shape[2]
    groups = LANES // width
    left = dot(xhat.T.astype(BF16), w_ref[:, :width])
    right = dot(w_ref[:, width:], xhat.astype(BF16), 0, 0).astype(BF16)
    for r in range(rows):
        starts = [(r * groups + k) * part for k in range(groups)]
        packed = jnp.concatenate([left[n : n + part] for n in starts], axis=1).astype(BF16)
        for c in range(cols):
            left_ref[r * cols + c] = packed
            right_ref[r * cols + c] = right[:, c * per_col : (c + 1) * per_col]


def arrange(left_ref, rows_ref, wide_ref):
    seqs, part, _ = left_ref.shape
    for s in range(seqs):
        wide_ref[s * part : (s + 1) * part, :] = left_ref[s].astype(F32)
    for p in range(part):
        block = wide_ref[pl.ds(p, seqs, stride=part), :]
        rows_ref[p * seqs : (p + 1) * seqs, :] = block.astype(BF16)


def unpack(block, width, steps):
    group = pl.program_id(0) // steps
    return pltpu.roll(block.astype(F32), lax.rem(LANES - group * width, LANES), 1)


def t_block(seqs, left, w_ref, t_ref):
    z = t_ref.shape[1] // (left.shape[0] // seqs)
    for e in range(0, w_ref.shape[1] // z, 2):
        o = (dot(left, w_ref[:, e * z : (e + 2) * z]) * (1.0 / seqs)).astype(BF16)
        for k in range(2):
            for i in range(left.shape[0] // seqs):
                t_ref[(e + k) * seqs : (e + k + 1) * seqs, i * z : (i + 1) * z] = o[
                    i * seqs : (i + 1) * seqs, k * z : (k + 1) * z
                ]


def u_block(seqs, rt_ref, g_ref, u_ref):
    step, _, z = g_ref.shape
    for p in range(0, step, 2):
        pair = jnp.concatenate([g_ref[p], g_ref[p + 1]], axis=1)
        for m in range(0, rt_ref.shape[0], 256):
            o = (dot(rt_ref[m : m + 256, :], pair) * (1.0 / seqs)).astype(BF16)
            for k in range(256 // seqs):
                e = m // seqs + k
                for h in range(2):
                    u_ref[(p + h) * seqs : (p + h + 1) * seqs, e * z : (e + 1) * z] = o[
                        k * seqs : (k + 1) * seqs, h * z : (h + 1) * z
                    ]


def pair_block(r_ref, t_ref, bias_ref, out_ref):
    z = out_ref.shape[2]
    for i in range(0, out_ref.shape[0], 2):
        o = dot(r_ref[...], t_ref[:, i * z : (i + 2) * z])
        for h in range(2):
            out_ref[i + h] = (o[:, h * z : (h + 1) * z] + bias_ref[...].astype(F32)).astype(BF16)


def right_block(t_ref, g_ref, acc_ref):
    grads = jnp.concatenate([g_ref[i] for i in range(g_ref.shape[0])], axis=1)
    for m in range(0, t_ref.shape[0], 256):
        o = dot(t_ref[m : m + 256, :], grads, 1, 1)
        for k in range(acc_ref.shape[0]):
            acc_ref[k, m : m + 256, :] += o[:, k * LANES : (k + 1) * LANES]


def right_flush(seqs, acc_ref, out_ref):
    for s in range(seqs):
        for k in range(acc_ref.shape[0]):
            block = acc_ref.at[k][pl.ds(s, out_ref.shape[1], stride=seqs), :]
            out_ref[s, :, k * LANES : (k + 1) * LANES] = block.astype(BF16)


def first():
    return pl.program_id(0) == 0


def last():
    return pl.program_id(0) == pl.num_programs(0) - 1


def step_rows(seqs, step, steps, rows_ref, width):
    size = step * seqs
    start = pl.multiple_of(lax.rem(pl.program_id(0), steps) * size, size)
    return unpack(rows_ref[pl.ds(start, size), :], width, steps)[:, :width].astype(BF16)


def widen(couple_ref, w_ref, wide_ref):
    width = w_ref.shape[0]
    z = couple_ref.shape[1]
    wide_ref[...] = couple_ref[...].astype(F32)
    for e in range(couple_ref.shape[0] // width):
        block = wide_ref[pl.ds(e, width, stride=width), :]
        w_ref[:, e * z : (e + 1) * z] = block.astype(BF16)


def block_in(t_ref, buf_ref, sem, n):
    slot = lax.rem(n, buf_ref.shape[0])
    return pltpu.make_async_copy(t_ref.at[n], buf_ref.at[slot], sem.at[slot])


def block_out(t_ref, buf_ref, sem, n):
    slot = lax.rem(n, buf_ref.shape[0])
    return pltpu.make_async_copy(buf_ref.at[slot], t_ref.at[n], sem.at[slot])


def stream(t_ref, buf_ref, sem):
    i, count, depth = pl.program_id(0), t_ref.shape[0], buf_ref.shape[0]

    @pl.when(first())
    def _():
        for n in range(depth - 1):
            block_in(t_ref, buf_ref, sem, n).start()

    @pl.when(i + depth - 1 < count)
    def _():
        block_in(t_ref, buf_ref, sem, i + depth - 1).start()

    block_in(t_ref, buf_ref, sem, i).wait()
    return buf_ref.at[lax.rem(i, depth)]


def t_kernel(
    seqs, step, steps, left_ref, couple_ref, rows_ref, w_ref, t_ref, wide_ref, tall_ref, buf_ref, sem
):
    i, count, depth = pl.program_id(0), t_ref.shape[0], buf_ref.shape[0]

    @pl.when(first())
    def _():
        arrange(left_ref, rows_ref, wide_ref)
        widen(couple_ref, w_ref, tall_ref)

    @pl.when(i >= depth)
    def _():
        block_out(t_ref, buf_ref, sem, i - depth).wait()

    left = step_rows(seqs, step, steps, rows_ref, w_ref.shape[0])
    t_block(seqs, left, w_ref, buf_ref.at[lax.rem(i, depth)])
    block_out(t_ref, buf_ref, sem, i).start()

    @pl.when(last())
    def _():
        for n in range(count - depth, count):
            block_out(t_ref, buf_ref, sem, n).wait()


def arrange_kernel(left_ref, couple_ref, rows_ref, w_ref, wide_ref, tall_ref):
    arrange(left_ref, rows_ref, wide_ref)
    widen(couple_ref, w_ref, tall_ref)


def arrange_right(all_ref, rt_ref, right_ref, wide_ref):
    seqs, width, jl = all_ref.shape
    for s in range(seqs):
        for k in range(jl // LANES):
            block = all_ref[s, :, k * LANES : (k + 1) * LANES]
            wide_ref[k, s * width : (s + 1) * width, :] = block.astype(F32)
    for e in range(width):
        for k in range(jl // LANES):
            block = wide_ref.at[k][pl.ds(e, seqs, stride=width), :]
            rt_ref[e * seqs : (e + 1) * seqs, k * LANES : (k + 1) * LANES] = block.astype(BF16)
    for n in range(0, width * seqs, LANES):
        right_ref[:, n : n + LANES] = rt_ref[n : n + LANES, :].astype(F32).T.astype(BF16)


def u_kernel(
    seqs, steps, rows_ref, all_ref, g_ref, w_ref, send_ref, right_ref, u_ref, dl_ref, dw_ref, rt_ref, wide_ref
):
    @pl.when(first())
    def _():
        arrange_right(all_ref, rt_ref, right_ref, wide_ref)
        dw_ref[...] = jnp.zeros_like(dw_ref)

    u_block(seqs, rt_ref, g_ref, u_ref)
    size, width, z = u_ref.shape[0], w_ref.shape[0], g_ref.shape[2]
    start = pl.multiple_of(pl.program_id(0) * size, size)
    dl_ref[pl.ds(start, size), :width] = dot(u_ref[...], w_ref[...], 1, 1)
    left_t = unpack(rows_ref[...], width, steps).T[:width].astype(BF16)
    for n in range(0, u_ref.shape[1], 512):
        dw_ref[:, n : n + 512] += dot(left_t, u_ref[:, n : n + 512])

    @pl.when(last())
    def _():
        share = send_ref.shape[1] - width
        per = width // share
        count = dl_ref.shape[0] // seqs
        for d in range(seqs):
            e, c = d // per, d % per * share
            block = dw_ref[c : c + share, e * z : (e + 1) * z]
            send_ref[d, width:, :] = block.astype(BF16)
            block = dl_ref[pl.ds(d, count, stride=seqs), :].T[:width]
            if count < LANES:
                block = jnp.concatenate([block, jnp.zeros((width, LANES - count), F32)], 1)
            send_ref[d, :width, :] = block.astype(BF16)


def right_kernel(seqs, t_ref, g_ref, out_ref, acc_ref, buf_ref, sem):
    block = stream(t_ref, buf_ref, sem)

    @pl.when(first())
    def _():
        acc_ref[...] = jnp.zeros_like(acc_ref)

    right_block(block, g_ref, acc_ref)

    @pl.when(last())
    def _():
        right_flush(seqs, acc_ref, out_ref)


def pair_kernel(r_ref, bias_ref, t_ref, out_ref, buf_ref, sem):
    pair_block(r_ref, stream(t_ref, buf_ref, sem), bias_ref, out_ref)


def fused_kernel(
    seqs, step, steps, rows_ref, w_ref, r_ref, g_ref, bias_ref, pair_out, out_ref, t_ref, acc_ref
):
    @pl.when(first())
    def _():
        acc_ref[...] = jnp.zeros_like(acc_ref)

    left = unpack(rows_ref[...], w_ref.shape[0], steps)[:, : w_ref.shape[0]].astype(BF16)
    t_block(seqs, left, w_ref, t_ref)
    right_block(t_ref, g_ref, acc_ref)
    pair_block(r_ref, t_ref, bias_ref, pair_out)

    @pl.when(last())
    def _():
        right_flush(seqs, acc_ref, out_ref)


def share_kernel(parts_ref, _, out_ref):
    share = parts_ref.shape[1]
    total = parts_ref[0].astype(F32)
    for d in range(1, parts_ref.shape[0]):
        total += parts_ref[d].astype(F32)
    for d in range(out_ref.shape[0]):
        out_ref[d, :share, :] = total.astype(BF16)


def finish_kernel(rows, cols, left_ref, right_ref, x_ref, w_ref, out_ref, weight_ref):
    width = left_ref.shape[1]
    jl = right_ref.shape[2] - LANES
    il = x_ref.shape[2] // rows
    lefts, rights = [], []
    for r in range(rows):
        terms = [left_ref[r * cols + c].astype(F32) for c in range(cols)]
        lefts.append(sum(terms[1:], terms[0])[:, :il])
    for c in range(cols):
        terms = [right_ref[r * cols + c, :, :jl].astype(F32) for r in range(rows)]
        rights.append(sum(terms[1:], terms[0]))
    both = jnp.concatenate([jnp.concatenate(lefts, 1), jnp.concatenate(rights, 1)], 0)
    grad = dot(w_ref[...], both.astype(BF16))
    xhat, rstd = normalize(x_ref[0].astype(F32))
    mean = jnp.mean(grad, axis=0, keepdims=True)
    proj = jnp.mean(grad * xhat, axis=0, keepdims=True)
    out_ref[0] = (rstd * (grad - mean - xhat * proj)).astype(BF16)
    share = width * width // (rows * cols)
    for d in range(rows * cols):
        e, c = d * share // width, d * share % width
        block = right_ref[d, :share, jl:].astype(F32)
        weight_ref[pl.ds(c * width + e, share, stride=width), :] = block


def on_device(x, split, couple, bias, cot):
    rows, cols = lax.axis_size("row"), lax.axis_size("col")
    seqs = rows * cols
    width = split.shape[1] // 2
    length, depth = x.shape[1], x.shape[2]
    il, jl, z = cot.shape
    part = il * width // LANES
    step = max(2, 256 // seqs)
    steps = part // step
    grid = (il // step,)
    shape = jax.ShapeDtypeStruct
    x_t = x.transpose(0, 2, 1)

    left_send, right_send = call(
        functools.partial(project_kernel, rows, cols),
        (1,),
        [whole(x_t.shape), whole(split.shape)],
        [
            (whole((seqs, part, LANES)), shape((seqs, part, LANES), BF16)),
            (whole((seqs, width, jl)), shape((seqs, width, jl), BF16)),
        ],
        [],
        2 * length * depth * depth,
        (x_t, split),
    )
    left_all = lax.all_to_all(left_send, AXES, 0, 0, tiled=True)
    right_all = lax.all_to_all(right_send, AXES, 0, 0, tiled=True)
    bias_row = bias[None, :]

    unit = 2 * il * jl * z * seqs * width
    small = 2 * il * seqs * width * width * z
    rows_spec = pl.BlockSpec((step * seqs, LANES), lambda i: (lax.rem(i, steps), 0))
    cot_spec = pl.BlockSpec((step, jl, z), lambda i: (i, 0, 0))
    arranged = [
        (whole((part * seqs, LANES)), shape((part * seqs, LANES), BF16)),
        (whole((width, width * z)), shape((width, width * z), BF16)),
    ]
    wides = [pltpu.VMEM((part * seqs, LANES), F32), pltpu.VMEM(couple.shape, F32)]
    t_shape = (il // step, width * seqs, step * z)
    depth = min(DEPTH, t_shape[0])
    any_spec = pl.BlockSpec(memory_space=pl.ANY)
    slots = [pltpu.VMEM((depth, *t_shape[1:]), BF16), pltpu.SemaphoreType.DMA((depth,))]
    stored = 2 * math.prod(t_shape) <= STORED_BYTES
    if stored:
        left_rows, weight, t_all = call(
            functools.partial(t_kernel, seqs, step, steps),
            grid,
            [whole(left_all.shape), whole(couple.shape)],
            arranged + [(any_spec, shape(t_shape, BF16))],
            wides + slots,
            small,
            (left_all, couple),
        )
        right_all, t_all = lax.optimization_barrier((right_all, t_all))
    else:
        left_rows, weight = call(
            arrange_kernel,
            (1,),
            [whole(left_all.shape), whole(couple.shape)],
            arranged,
            wides,
            0,
            (left_all, couple),
        )
    share = width * width // seqs
    right_shape = (jl, width * seqs)
    send_one, right = call(
        functools.partial(u_kernel, seqs, steps),
        grid,
        [rows_spec, whole(right_all.shape), cot_spec, whole(weight.shape)],
        [
            (
                whole((seqs, width + share, LANES)),
                shape((seqs, width + share, LANES), BF16),
            ),
            (whole(right_shape), shape(right_shape, BF16)),
        ],
        [
            pltpu.VMEM((step * seqs, width * z), BF16),
            pltpu.VMEM((il * seqs, LANES), F32),
            pltpu.VMEM((width, width * z), F32),
            pltpu.VMEM((width * seqs, jl), BF16),
            pltpu.VMEM((jl // LANES, width * seqs, LANES), F32),
        ],
        unit + 2 * small,
        (left_rows, right_all, cot, weight),
    )
    got_one = lax.all_to_all(send_one, AXES, 0, 0, tiled=True)
    right_out = (whole((seqs, width, jl)), shape((seqs, width, jl + LANES), BF16))
    acc = pltpu.VMEM((jl // LANES, width * seqs, LANES), F32)
    if stored:
        (right_back,) = call(
            functools.partial(right_kernel, seqs),
            grid,
            [any_spec, cot_spec],
            [right_out],
            [acc] + slots,
            unit,
            (t_all, cot),
        )
        (pair,) = call(
            pair_kernel,
            grid,
            [whole(right.shape), whole(bias_row.shape), any_spec],
            [(cot_spec, shape(cot.shape, BF16))],
            slots,
            unit,
            (right, bias_row, t_all),
        )
    else:
        pair, right_back = call(
            functools.partial(fused_kernel, seqs, step, steps),
            grid,
            [rows_spec, whole(weight.shape), whole(right.shape), cot_spec, whole(bias_row.shape)],
            [(cot_spec, shape(cot.shape, BF16)), right_out],
            [pltpu.VMEM((width * seqs, step * z), BF16), acc],
            2 * unit + small,
            (left_rows, weight, right, cot, bias_row),
        )
    (send_two,) = call(
        share_kernel,
        (1,),
        [
            pl.BlockSpec((seqs, share, LANES), lambda i: (0, width // share, 0)),
            pl.BlockSpec(memory_space=pl.ANY),
        ],
        [
            (
                pl.BlockSpec((seqs, width, LANES), lambda i: (0, 0, jl // LANES)),
                shape(right_back.shape, BF16),
            )
        ],
        [],
        0,
        (got_one, right_back),
        {1: 0},
    )
    got_two = lax.all_to_all(send_two, AXES, 0, 0, tiled=True)
    align, weight_grad = call(
        functools.partial(finish_kernel, rows, cols),
        (1,),
        [
            pl.BlockSpec((seqs, width, LANES), lambda i: (0, 0, 0)),
            whole(got_two.shape),
            whole(x_t.shape),
            whole(split.shape),
        ],
        [
            (whole(x_t.shape), shape(x_t.shape, BF16)),
            (whole((width * width, z)), shape((width * width, z), F32)),
        ],
        [],
        2 * length * depth * depth,
        (got_one, got_two, x_t, split),
    )
    return pair, align.transpose(0, 2, 1), weight_grad


def solution(mesh):
    placed = (P(AXES, None, None), P(), P(), P(), P("row", "col", None))
    return jax.shard_map(
        on_device,
        mesh=mesh,
        in_specs=placed,
        out_specs=(P("row", "col", None), P(AXES, None, None), P()),
        check_vma=False,
    )
```

time: 940 us -> 134 us (0.14); the launches traced: 929 us -> 133 us
  local copies, waits for them, and re-layouts: 410 us -> 2.49 us
  matrix products: 274 us -> 0 us
  waiting for transfers between devices: 161 us -> 4.93 us
  Pallas kernels: 0 us -> 93.2 us
  loops' own time: 20.7 us -> 0 us
  between operations: 16.1 us -> 0.71 us
    dot_general x50 -> x0, matrix products: 274 us -> none  [the longest x8 67 us: advance(): jnp.einsum('ijce,sic->sje', outer_grad, left_block, preferred_element_typ...]
    convert_element_type x19 -> x0, local copies, waits for them, and re-layouts: 187 us -> none  [the longest x8 91.1 us: advance(): jnp.dot(grad_rows, weight_back, preferred_element_type=jnp.float32)]
    while x65 -> x0, local copies, waits for them, and re-layouts: 177 us -> none
    pallas_call x0 -> x7, Pallas kernels: none -> 93.2 us  [call(): pl.pallas_call(kernel, grid_spec=pltpu.PrefetchScalarGridSpec(num_scalar_...]
    psum x1 -> x0, waiting for transfers between devices: 87.1 us -> none  [on_device(): factor_weight_gradient = lax.psum(weight_part, ('row', 'col'))]
    reduce_scatter x2 -> x0, waiting for transfers between devices: 42.8 us -> none  [the longest x1 39.1 us: on_device(): lax.psum_scatter(right_home, 'row', scatter_dimension=0, tiled=True)]
    all_to_all x4 -> x3, waiting for transfers between devices: 30.8 us -> 4.93 us  [the longest x1 4.92 us: on_device(): got_two = lax.all_to_all(send_two, AXES, 0, 0, tiled=True)]
    all_gather x2 -> x0, blocking collectives: 24.4 us -> none  [the longest x1 13.3 us: on_device(): left_all = lax.all_gather(left, 'col', axis=0, tiled=True)]
  transfers between devices with their start and end apart: 7 -> 3, of which waited for: 6 -> 1; matrix products, arithmetic and copies ran while one was open for 1% -> 0% of each run, Pallas kernels for 0% -> 40%
where the time goes in v1:
time: 134 us; the launch traced here: 133 us
  Pallas kernels  93.2 us (70%)
  blocking collectives  17.5 us (13%)
  starting transfers between devices  14.2 us (11%)
  waiting for transfers between devices  4.93 us (4%)
  local copies, waits for them, and re-layouts  2.49 us (2%)
    pallas_call x7, Pallas kernels, call(): pl.pallas_call(kernel, grid_spec=pltpu.PrefetchScalarGridSpec(num_scalar_...  93.2 us
    all_to_all x1, blocking collectives, on_device(): left_all = lax.all_to_all(left_send, AXES, 0, 0, tiled=True)  17.5 us
    all_to_all x1, starting transfers between devices, on_device(): got_two = lax.all_to_all(send_two, AXES, 0, 0, tiled=True)  5.84 us
    all_to_all x1, starting transfers between devices, on_device(): got_one = lax.all_to_all(send_one, AXES, 0, 0, tiled=True)  5.83 us
    all_to_all x1, waiting for transfers between devices, on_device(): got_two = lax.all_to_all(send_two, AXES, 0, 0, tiled=True)  4.92 us
  transfers between devices with their start and end apart: 3, of which 1 were waited for; matrix products, arithmetic and copies ran while one was open for 0% of the time, Pallas kernels for 40%

profile of v1, /device:TPU:1, one launch (start us, length us, event | category | flops | bytes accessed | tf_op | source)
XLA Modules:
  0.0 133.1 jit_solution(4303059517352459453)
XLA Ops:
  0.6 2.2 %shard_map.76 = (bf16[32,32,128]{2,1,0:T(8,128)(2,1)}, bf16[32,32,256]{2,1,0:T(8,128)(2,1)}) custom-call(bf16[1,64,1024]{2,1,0:T(8,128)(2,1)} %bitcast.3, bf16[64,64]{1,0:T(8,128)(2,1)} %w_ref.3), custom_call_target="tpu_custom_call" | custom-call | flops 8388608 | bytes 925696 | tf_op jit(solution)/shard_map/pallas_call | solution.py:31
  2.8 17.5 %all_to_all.20.left_ref = bf16[32,32,128]{2,1,0:T(8,128)(2,1)} all-to-all(bf16[32,32,128]{2,1,0:T(8,128)(2,1)} %get-tuple-element.14), channel_id=1, replica_groups=mesh['row'=8,'col'=4] {'row','col'}, dimensions={0} | all-to-all | bytes 524288 | tf_op jit(solution)/shard_map/all_to_all | solution.py:347
  20.3 2.6 %all-to-all-start.1 = ((bf16[32,32,256]{2,1,0:T(8,128)(2,1)}), bf16[32,32,256]{2,1,0:T(8,128)(2,1)S(1)}, u32[]{:S(2)}, u32[]{:S(2)}) async-start(bf16[32,32,256]{2,1,0:T(8,128)(2,1)} %get-tuple-element.16), calls=%async_computation.1 | async-start | bytes 1048576 | tf_op jit(solution)/shard_map/all_to_all | solution.py:348
  22.9 17.8 %shard_map.77 = (bf16[1024,128]{1,0:T(8,128)(2,1)}, bf16[32,4096]{1,0:T(8,128)(2,1)}, bf16[16,1024,1024]{2,1,0:T(8,128)(2,1)}) custom-call(bf16[32,32,128]{2,1,0:T(8,128)(2,1)} %all_to_all.20.left_ref, bf16[1024,128]{1,0:T(8,128)(2,1)} %couple_ref.1), custom_call_target="tpu_custom_call" | custom-call | flops 1073741824 | bytes 34603008 | tf_op jit(solution)/shard_map/pallas_call | solution.py:31
  40.7 0.0 all-to-all-done.1.all_ref
  40.7 0.0 copy-start.2
  40.8 0.8 copy-done.2
  41.5 33.3 %shard_map.78 = (bf16[32,64,128]{2,1,0:T(8,128)(2,1)}, bf16[256,1024]{1,0:T(8,128)(2,1)}) custom-call(bf16[1024,128]{1,0:T(8,128)(2,1)} %get-tuple-element.15.rows_ref, bf16[32,32,256]{2,1,0:T(8,128)(2,1)} %copy-done.2, bf16[128,256,128]{2,1,0:T(8,128)(2,1)} %g_ref.3, bf16[32,4096]{1,0:T(8,128)(2,1)} %get-tuple-element.19.w_ref), custom_call_target="tpu_custom_call" | custom-call | flops 10737418240 | bytes 10485760 | tf_op jit(solution)/shard_map/pallas_call | solution.py:31
  74.8 5.8 %all-to-all-start.2 = ((bf16[32,64,128]{2,1,0:T(8,128)(2,1)}), bf16[32,64,128]{2,1,0:T(8,128)(2,1)S(1)}, u32[]{:S(2)}, u32[]{:S(2)}) async-start(bf16[32,64,128]{2,1,0:T(8,128)(2,1)} %get-tuple-element.22), calls=%async_computation.2 | async-start | bytes 1048576 | tf_op jit(solution)/shard_map/all_to_all | solution.py:409
  80.7 19.5 %shard_map.80._ = bf16[32,32,384]{2,1,0:T(8,128)(2,1)} custom-call(bf16[16,1024,1024]{2,1,0:T(8,128)(2,1)} %get-tuple-element.21.t_ref, bf16[128,256,128]{2,1,0:T(8,128)(2,1)} %g_ref.3), custom_call_target="tpu_custom_call" | custom-call | flops 8589934592 | bytes 42729472 | tf_op jit(solution)/shard_map/pallas_call | solution.py:31
  100.2 0.0 all-to-all-done.2.parts_ref.left_ref
  100.2 0.0 copy-start
  100.2 0.8 copy-done
  101.1 1.8 %shard_map.81 = bf16[32,32,384]{2,1,0:T(8,128)(2,1)} custom-call(bf16[32,64,128]{2,1,0:T(8,128)(2,1)} %copy-done, bf16[32,32,384]{2,1,0:T(8,128)(2,1)} %shard_map.80._), custom_call_target="tpu_custom_call", output_to_operand_aliasing={{}: (1, {})} | custom-call | bytes 2097152 | tf_op jit(solution)/shard_map/pallas_call | solution.py:31
  102.8 5.8 %all-to-all-start.3 = ((bf16[32,32,384]{2,1,0:T(8,128)(2,1)}), bf16[32,32,384]{2,1,0:T(8,128)(2,1)S(1)}, u32[]{:S(2)}, u32[]{:S(2)}) async-start(bf16[32,32,384]{2,1,0:T(8,128)(2,1)} %shard_map.81), calls=%async_computation.3 | async-start | bytes 1572864 | tf_op jit(solution)/shard_map/all_to_all | solution.py:459
  108.7 15.9 %shard_map.79 = bf16[128,256,128]{2,1,0:T(8,128)(2,1)} custom-call(bf16[256,1024]{1,0:T(8,128)(2,1)} %get-tuple-element.20.r_ref, bf16[1,128]{1,0:T(2,128)(2,1)} %bitcast.5, bf16[16,1024,1024]{2,1,0:T(8,128)(2,1)} %get-tuple-element.21.t_ref), custom_call_target="tpu_custom_call" | custom-call | flops 8589934592 | bytes 42467584 | tf_op jit(solution)/shard_map/pallas_call | solution.py:31
  124.5 4.9 %all-to-all-done.3.right_ref = bf16[32,32,384]{2,1,0:T(8,128)(2,1)S(1)} async-done(((bf16[32,32,384]{2,1,0:T(8,128)(2,1)}), bf16[32,32,384]{2,1,0:T(8,128)(2,1)S(1)}, u32[]{:S(2)}, u32[]{:S(2)}) %all-to-all-start.3) | async-done | bytes 786464 | tf_op jit(solution)/shard_map/all_to_all | solution.py:459
  129.5 0.0 copy-start.1
  129.5 0.9 copy-done.1
  130.4 2.8 %shard_map.82 = (bf16[1,64,1024]{2,1,0:T(8,128)(2,1)}, f32[1024,128]{1,0:T(8,128)}) custom-call(bf16[32,64,128]{2,1,0:T(8,128)(2,1)} %copy-done, bf16[32,32,384]{2,1,0:T(8,128)(2,1)} %copy-done.1, bf16[1,64,1024]{2,1,0:T(8,128)(2,1)} %bitcast.4, bf16[64,64]{1,0:T(8,128)(2,1)} %w_ref.3), custom_call_target="tpu_custom_call" | custom-call | flops 32768 | bytes 2105344 | tf_op jit(solution)/shard_map/pallas_call | solution.py:31
Async XLA Ops:
  20.3 20.4 %all-to-all-start.1 = ((bf16[32,32,256]{2,1,0:T(8,128)(2,1)}), bf16[32,32,256]{2,1,0:T(8,128)(2,1)S(1)}, u32[]{:S(2)}, u32[]{:S(2)}) async-start(bf16[32,32,256]{2,1,0:T(8,128)(2,1)} %get-tuple-element.16), calls=%async_computation.1 | async-start | bytes 1048576 | tf_op jit(solution)/shard_map/all_to_all | solution.py:348
  40.7 0.8 copy-start.2
  74.8 25.4 %all-to-all-start.2 = ((bf16[32,64,128]{2,1,0:T(8,128)(2,1)}), bf16[32,64,128]{2,1,0:T(8,128)(2,1)S(1)}, u32[]{:S(2)}, u32[]{:S(2)}) async-start(bf16[32,64,128]{2,1,0:T(8,128)(2,1)} %get-tuple-element.22), calls=%async_computation.2 | async-start | bytes 1048576 | tf_op jit(solution)/shard_map/all_to_all | solution.py:409
  100.2 0.8 copy-start
  102.8 26.6 %all-to-all-start.3 = ((bf16[32,32,384]{2,1,0:T(8,128)(2,1)}), bf16[32,32,384]{2,1,0:T(8,128)(2,1)S(1)}, u32[]{:S(2)}, u32[]{:S(2)}) async-start(bf16[32,32,384]{2,1,0:T(8,128)(2,1)} %shard_map.81), calls=%async_computation.3 | async-start | bytes 1572864 | tf_op jit(solution)/shard_map/all_to_all | solution.py:459
  129.5 0.9 copy-start.1

commit v2 on v1

--- a/solution.py
+++ b/solution.py
@@ -13,7 +13,9 @@
 AXES = ("row", "col")
 LANES = 128
 VMEM_BYTES = 56 << 20
-DEPTH = 4
+DEPTH = 3
+SMALL_BYTES = 24 << 20
+U_BYTES = 48 << 20
 STORED_BYTES = 1 << 25
 
 
@@ -25,7 +27,11 @@
     return pl.BlockSpec(shape, lambda *_: (0,) * len(shape))
 
 
-def call(kernel, grid, ins, outs, scratch, flops, args, aliases={}):
+def in_hbm(a):
+    return pltpu.with_memory_space_constraint(a, pltpu.HBM)
+
+
+def call(kernel, grid, ins, outs, scratch, flops, args, aliases={}, limit=VMEM_BYTES):
     nbytes = sum(a.size * a.dtype.itemsize for a in args)
     nbytes += sum(math.prod(o.shape) * o.dtype.itemsize for _, o in outs)
     return pl.pallas_call(
@@ -39,7 +45,7 @@
         ),
         out_shape=[o for _, o in outs],
         input_output_aliases=aliases,
-        compiler_params=pltpu.CompilerParams(vmem_limit_bytes=VMEM_BYTES),
+        compiler_params=pltpu.CompilerParams(vmem_limit_bytes=limit),
         cost_estimate=pl.CostEstimate(flops=flops, bytes_accessed=nbytes, transcendentals=0),
     )(*args)
 
@@ -326,7 +332,7 @@
     length, depth = x.shape[1], x.shape[2]
     il, jl, z = cot.shape
     part = il * width // LANES
-    step = max(2, 256 // seqs)
+    step = max(2, 512 // seqs)
     steps = part // step
     grid = (il // step,)
     shape = jax.ShapeDtypeStruct
@@ -353,8 +359,8 @@
     rows_spec = pl.BlockSpec((step * seqs, LANES), lambda i: (lax.rem(i, steps), 0))
     cot_spec = pl.BlockSpec((step, jl, z), lambda i: (i, 0, 0))
     arranged = [
-        (whole((part * seqs, LANES)), shape((part * seqs, LANES), BF16)),
-        (whole((width, width * z)), shape((width, width * z), BF16)),
+        (whole((part * seqs, LANES)), pltpu.HBM((part * seqs, LANES), BF16)),
+        (whole((width, width * z)), pltpu.HBM((width, width * z), BF16)),
     ]
     wides = [pltpu.VMEM((part * seqs, LANES), F32), pltpu.VMEM(couple.shape, F32)]
     t_shape = (il // step, width * seqs, step * z)
@@ -384,6 +390,7 @@
             (left_all, couple),
         )
     share = width * width // seqs
+    left_rows, weight = in_hbm(left_rows), in_hbm(weight)
     right_shape = (jl, width * seqs)
     send_one, right = call(
         functools.partial(u_kernel, seqs, steps),
@@ -394,7 +401,7 @@
                 whole((seqs, width + share, LANES)),
                 shape((seqs, width + share, LANES), BF16),
             ),
-            (whole(right_shape), shape(right_shape, BF16)),
+            (whole(right_shape), pltpu.HBM(right_shape, BF16)),
         ],
         [
             pltpu.VMEM((step * seqs, width * z), BF16),
@@ -405,9 +412,10 @@
         ],
         unit + 2 * small,
         (left_rows, right_all, cot, weight),
+        limit=U_BYTES,
     )
     got_one = lax.all_to_all(send_one, AXES, 0, 0, tiled=True)
-    right_out = (whole((seqs, width, jl)), shape((seqs, width, jl + LANES), BF16))
+    right_out = (whole((seqs, width, jl)), pltpu.HBM((seqs, width, jl + LANES), BF16))
     acc = pltpu.VMEM((jl // LANES, width * seqs, LANES), F32)
     if stored:
         (right_back,) = call(
@@ -448,13 +456,14 @@
         [
             (
                 pl.BlockSpec((seqs, width, LANES), lambda i: (0, 0, jl // LANES)),
-                shape(right_back.shape, BF16),
+                pltpu.HBM(right_back.shape, BF16),
             )
         ],
         [],
         0,
-        (got_one, right_back),
+        (got_one, in_hbm(right_back)),
         {1: 0},
+        SMALL_BYTES,
     )
     got_two = lax.all_to_all(send_two, AXES, 0, 0, tiled=True)
     align, weight_grad = call(
@@ -473,6 +482,7 @@
         [],
         2 * length * depth * depth,
         (got_one, got_two, x_t, split),
+        limit=SMALL_BYTES,
     )
     return pair, align.transpose(0, 2, 1), weight_grad
 

time: 134 us -> 120 us (0.90)
  Pallas kernels: 93.2 us -> 83.1 us
  local copies, waits for them, and re-layouts: 2.49 us -> 0.01 us
    pallas_call x7, Pallas kernels: 93.2 us -> 83.1 us  [call(): pl.pallas_call(kernel, grid_spec=pltpu.PrefetchScalarGridSpec(num_scalar_...]
    unnamed x6 -> x4, local copies, waits for them, and re-layouts: 2.49 us -> 0.01 us
  transfers between devices with their start and end apart: 3 -> 3, of which waited for: 1 -> 1; matrix products, arithmetic and copies ran while one was open for 0% -> 0% of each run, Pallas kernels for 40% -> 41%
where the time goes in v2:
time: 120 us
  Pallas kernels  83.1 us (69%)
  blocking collectives  17.5 us (15%)
  starting transfers between devices  14.2 us (12%)
  waiting for transfers between devices  4.38 us (4%)
    pallas_call x7, Pallas kernels, call(): pl.pallas_call(kernel, grid_spec=pltpu.PrefetchScalarGridSpec(num_scalar_...  83.1 us
    all_to_all x1, blocking collectives, on_device(): left_all = lax.all_to_all(left_send, AXES, 0, 0, tiled=True)  17.5 us
    all_to_all x1, starting transfers between devices, on_device(): got_two = lax.all_to_all(send_two, AXES, 0, 0, tiled=True)  5.83 us
    all_to_all x1, starting transfers between devices, on_device(): got_one = lax.all_to_all(send_one, AXES, 0, 0, tiled=True)  5.83 us
    all_to_all x1, waiting for transfers between devices, on_device(): got_two = lax.all_to_all(send_two, AXES, 0, 0, tiled=True)  4.37 us
    all_to_all x1, starting transfers between devices, on_device(): right_all = lax.all_to_all(right_send, AXES, 0, 0, tiled=True)  2.57 us
  transfers between devices with their start and end apart: 3, of which 1 were waited for; matrix products, arithmetic and copies ran while one was open for 0% of the time, Pallas kernels for 41%

profile of v2, /device:TPU:1, one launch (start us, length us, event | category | flops | bytes accessed | tf_op | source)
XLA Modules:
  0.0 120.0 jit_solution(816920466923643470)
XLA Ops:
  0.6 2.2 %shard_map.76 = (bf16[32,32,128]{2,1,0:T(8,128)(2,1)}, bf16[32,32,256]{2,1,0:T(8,128)(2,1)}) custom-call(bf16[1,64,1024]{2,1,0:T(8,128)(2,1)} %bitcast.3, bf16[64,64]{1,0:T(8,128)(2,1)} %w_ref.3), custom_call_target="tpu_custom_call" | custom-call | flops 8388608 | bytes 925696 | tf_op jit(solution)/shard_map/pallas_call | solution.py:37
  2.8 17.5 %all_to_all.20.left_ref = bf16[32,32,128]{2,1,0:T(8,128)(2,1)} all-to-all(bf16[32,32,128]{2,1,0:T(8,128)(2,1)} %get-tuple-element.14), channel_id=1, replica_groups=mesh['row'=8,'col'=4] {'row','col'}, dimensions={0} | all-to-all | bytes 524288 | tf_op jit(solution)/shard_map/all_to_all | solution.py:353
  20.3 2.6 %all-to-all-start.1 = ((bf16[32,32,256]{2,1,0:T(8,128)(2,1)}), bf16[32,32,256]{2,1,0:T(8,128)(2,1)S(1)}, u32[]{:S(2)}, u32[]{:S(2)}) async-start(bf16[32,32,256]{2,1,0:T(8,128)(2,1)} %get-tuple-element.16), calls=%async_computation.1 | async-start | bytes 1048576 | tf_op jit(solution)/shard_map/all_to_all | solution.py:354
  22.9 16.5 %shard_map.77 = (bf16[1024,128]{1,0:T(8,128)(2,1)}, bf16[32,4096]{1,0:T(8,128)(2,1)}, bf16[8,1024,2048]{2,1,0:T(8,128)(2,1)}) custom-call(bf16[32,32,128]{2,1,0:T(8,128)(2,1)} %all_to_all.20.left_ref, bf16[1024,128]{1,0:T(8,128)(2,1)} %couple_ref.1), custom_call_target="tpu_custom_call" | custom-call | flops 1073741824 | bytes 34603008 | tf_op jit(solution)/shard_map/pallas_call | solution.py:37
  39.5 0.0 all-to-all-done.1.all_ref
  39.5 29.1 %shard_map.78 = (bf16[32,64,128]{2,1,0:T(8,128)(2,1)}, bf16[256,1024]{1,0:T(8,128)(2,1)}) custom-call(bf16[1024,128]{1,0:T(8,128)(2,1)} %get-tuple-element.15.rows_ref, bf16[32,32,256]{2,1,0:T(8,128)(2,1)S(1)} %all-to-all-done.1.all_ref, bf16[128,256,128]{2,1,0:T(8,128)(2,1)} %g_ref.3, bf16[32,4096]{1,0:T(8,128)(2,1)} %get-tuple-element.19.w_ref), custom_call_target="tpu_custom_call" | custom-call | flops 10737418240 | bytes 10485760 | tf_op jit(solution)/shard_map/pallas_call | solution.py:37
  68.6 5.8 %all-to-all-start.2 = ((bf16[32,64,128]{2,1,0:T(8,128)(2,1)}), bf16[32,64,128]{2,1,0:T(8,128)(2,1)S(1)}, u32[]{:S(2)}, u32[]{:S(2)}) async-start(bf16[32,64,128]{2,1,0:T(8,128)(2,1)} %get-tuple-element.22), calls=%async_computation.2 | async-start | bytes 1048576 | tf_op jit(solution)/shard_map/all_to_all | solution.py:417
  74.4 16.5 %shard_map.80._ = bf16[32,32,384]{2,1,0:T(8,128)(2,1)} custom-call(bf16[8,1024,2048]{2,1,0:T(8,128)(2,1)} %get-tuple-element.21.t_ref, bf16[128,256,128]{2,1,0:T(8,128)(2,1)} %g_ref.3), custom_call_target="tpu_custom_call" | custom-call | flops 8589934592 | bytes 42729472 | tf_op jit(solution)/shard_map/pallas_call | solution.py:37
  91.0 0.0 all-to-all-done.2.parts_ref.left_ref
  91.0 0.8 shard_map.81
  91.8 5.8 %all-to-all-start.3 = ((bf16[32,32,384]{2,1,0:T(8,128)(2,1)}), bf16[32,32,384]{2,1,0:T(8,128)(2,1)S(1)}, u32[]{:S(2)}, u32[]{:S(2)}) async-start(bf16[32,32,384]{2,1,0:T(8,128)(2,1)} %shard_map.81), calls=%async_computation.3 | async-start | bytes 1572864 | tf_op jit(solution)/shard_map/all_to_all | solution.py:468
  97.6 0.0 copy-start
  97.6 0.0 copy-start.1
  97.6 16.4 %shard_map.79 = bf16[128,256,128]{2,1,0:T(8,128)(2,1)} custom-call(bf16[256,1024]{1,0:T(8,128)(2,1)} %get-tuple-element.20.r_ref, bf16[1,128]{1,0:T(2,128)(2,1)} %bitcast.5, bf16[8,1024,2048]{2,1,0:T(8,128)(2,1)} %get-tuple-element.21.t_ref), custom_call_target="tpu_custom_call" | custom-call | flops 8589934592 | bytes 42467584 | tf_op jit(solution)/shard_map/pallas_call | solution.py:37
  114.0 4.4 %all-to-all-done.3.right_ref = bf16[32,32,384]{2,1,0:T(8,128)(2,1)S(1)} async-done(((bf16[32,32,384]{2,1,0:T(8,128)(2,1)}), bf16[32,32,384]{2,1,0:T(8,128)(2,1)S(1)}, u32[]{:S(2)}, u32[]{:S(2)}) %all-to-all-start.3) | async-done | bytes 786464 | tf_op jit(solution)/shard_map/all_to_all | solution.py:468
  118.4 0.0 copy-done
  118.4 0.0 copy-done.1
  118.4 1.6 %shard_map.82 = (bf16[1,64,1024]{2,1,0:T(8,128)(2,1)}, f32[1024,128]{1,0:T(8,128)}) custom-call(bf16[32,64,128]{2,1,0:T(8,128)(2,1)S(1)} %all-to-all-done.2.parts_ref.left_ref, bf16[32,32,384]{2,1,0:T(8,128)(2,1)S(1)} %all-to-all-done.3.right_ref, bf16[1,64,1024]{2,1,0:T(8,128)(2,1)S(1)} %bitcast.4, bf16[64,64]{1,0:T(8,128)(2,1)S(1)} %copy-done.1), custom_call_target="tpu_custom_call" | custom-call | flops 18432 | bytes 2105344 | tf_op jit(solution)/shard_map/pallas_call | solution.py:37
Async XLA Ops:
  20.3 19.1 %all-to-all-start.1 = ((bf16[32,32,256]{2,1,0:T(8,128)(2,1)}), bf16[32,32,256]{2,1,0:T(8,128)(2,1)S(1)}, u32[]{:S(2)}, u32[]{:S(2)}) async-start(bf16[32,32,256]{2,1,0:T(8,128)(2,1)} %get-tuple-element.16), calls=%async_computation.1 | async-start | bytes 1048576 | tf_op jit(solution)/shard_map/all_to_all | solution.py:354
  68.6 22.4 %all-to-all-start.2 = ((bf16[32,64,128]{2,1,0:T(8,128)(2,1)}), bf16[32,64,128]{2,1,0:T(8,128)(2,1)S(1)}, u32[]{:S(2)}, u32[]{:S(2)}) async-start(bf16[32,64,128]{2,1,0:T(8,128)(2,1)} %get-tuple-element.22), calls=%async_computation.2 | async-start | bytes 1048576 | tf_op jit(solution)/shard_map/all_to_all | solution.py:417
  91.8 26.6 %all-to-all-start.3 = ((bf16[32,32,384]{2,1,0:T(8,128)(2,1)}), bf16[32,32,384]{2,1,0:T(8,128)(2,1)S(1)}, u32[]{:S(2)}, u32[]{:S(2)}) async-start(bf16[32,32,384]{2,1,0:T(8,128)(2,1)} %shard_map.81), calls=%async_computation.3 | async-start | bytes 1572864 | tf_op jit(solution)/shard_map/all_to_all | solution.py:468
  97.6 20.8 %copy-start = (bf16[1,1024,64]{1,2,0:T(8,128)(2,1)S(1)}, bf16[1,1024,64]{1,2,0:T(8,128)(2,1)}, u32[]{:S(2)}) copy-start(bf16[1,1024,64]{1,2,0:T(8,128)(2,1)} %param.5) | copy-start | bytes 393220
  97.6 20.8 %copy-start.1 = (bf16[64,64]{1,0:T(8,128)(2,1)S(1)}, bf16[64,64]{1,0:T(8,128)(2,1)}, u32[]{:S(2)}) copy-start(bf16[64,64]{1,0:T(8,128)(2,1)} %w_ref.3) | copy-start | bytes 24580

commit v3 on v2

--- a/solution.py
+++ b/solution.py
@@ -25,6 +25,10 @@
 
 def whole(shape):
     return pl.BlockSpec(shape, lambda *_: (0,) * len(shape))
+
+
+def lanes(blocks):
+    return jnp.concatenate(list(blocks), axis=1)
 
 
 def in_hbm(a):
@@ -57,18 +61,26 @@
     return (x - mu) * rstd, rstd
 
 
-def project_kernel(rows, cols, x_ref, w_ref, left_ref, right_ref):
+def left_kernel(rows, cols, x_ref, w_ref, left_ref):
     xhat, _ = normalize(x_ref[0].astype(F32))
     width = w_ref.shape[1] // 2
-    part, per_col = left_ref.shape[1], right_ref.shape[2]
+    part = left_ref.shape[1]
     groups = LANES // width
     left = dot(xhat.T.astype(BF16), w_ref[:, :width])
+    for r in range(rows):
+        starts = [(r * groups + k) * part for k in range(groups)]
+        packed = lanes(left[n : n + part] for n in starts).astype(BF16)
+        for c in range(cols):
+            left_ref[r * cols + c] = packed
+
+
+def project_right_kernel(rows, cols, x_ref, w_ref, right_ref):
+    xhat, _ = normalize(x_ref[0].astype(F32))
+    width = w_ref.shape[1] // 2
+    per_col = right_ref.shape[2]
     right = dot(w_ref[:, width:], xhat.astype(BF16), 0, 0).astype(BF16)
     for r in range(rows):
-        starts = [(r * groups + k) * part for k in range(groups)]
-        packed = jnp.concatenate([left[n : n + part] for n in starts], axis=1).astype(BF16)
         for c in range(cols):
-            left_ref[r * cols + c] = packed
             right_ref[r * cols + c] = right[:, c * per_col : (c + 1) * per_col]
 
 
@@ -87,12 +99,12 @@
 
 
 def t_block(seqs, left, w_ref, t_ref):
-    z = t_ref.shape[1] // (left.shape[0] // seqs)
+    z = t_ref.shape[2]
     for e in range(0, w_ref.shape[1] // z, 2):
         o = (dot(left, w_ref[:, e * z : (e + 2) * z]) * (1.0 / seqs)).astype(BF16)
         for k in range(2):
             for i in range(left.shape[0] // seqs):
-                t_ref[(e + k) * seqs : (e + k + 1) * seqs, i * z : (i + 1) * z] = o[
+                t_ref[i, (e + k) * seqs : (e + k + 1) * seqs, :] = o[
                     i * seqs : (i + 1) * seqs, k * z : (k + 1) * z
                 ]
 
@@ -101,12 +113,13 @@
     step, _, z = g_ref.shape
     for p in range(0, step, 2):
         pair = jnp.concatenate([g_ref[p], g_ref[p + 1]], axis=1)
-        for m in range(0, rt_ref.shape[0], 256):
-            o = (dot(rt_ref[m : m + 256, :], pair) * (1.0 / seqs)).astype(BF16)
+        for m in range(0, rt_ref.shape[1], 256):
+            right = lanes(rt_ref[k, m : m + 256, :] for k in range(rt_ref.shape[0]))
+            o = (dot(right, pair) * (1.0 / seqs)).astype(BF16)
             for k in range(256 // seqs):
                 e = m // seqs + k
                 for h in range(2):
-                    u_ref[(p + h) * seqs : (p + h + 1) * seqs, e * z : (e + 1) * z] = o[
+                    u_ref[e, (p + h) * seqs : (p + h + 1) * seqs, :] = o[
                         k * seqs : (k + 1) * seqs, h * z : (h + 1) * z
                     ]
 
@@ -114,15 +127,16 @@
 def pair_block(r_ref, t_ref, bias_ref, out_ref):
     z = out_ref.shape[2]
     for i in range(0, out_ref.shape[0], 2):
-        o = dot(r_ref[...], t_ref[:, i * z : (i + 2) * z])
+        right = lanes(r_ref[n] for n in range(r_ref.shape[0]))
+        o = dot(right, lanes((t_ref[i], t_ref[i + 1])))
         for h in range(2):
             out_ref[i + h] = (o[:, h * z : (h + 1) * z] + bias_ref[...].astype(F32)).astype(BF16)
 
 
 def right_block(t_ref, g_ref, acc_ref):
     grads = jnp.concatenate([g_ref[i] for i in range(g_ref.shape[0])], axis=1)
-    for m in range(0, t_ref.shape[0], 256):
-        o = dot(t_ref[m : m + 256, :], grads, 1, 1)
+    for m in range(0, t_ref.shape[1], 256):
+        o = dot(lanes(t_ref[i, m : m + 256, :] for i in range(t_ref.shape[0])), grads, 1, 1)
         for k in range(acc_ref.shape[0]):
             acc_ref[k, m : m + 256, :] += o[:, k * LANES : (k + 1) * LANES]
 
@@ -221,9 +235,11 @@
     for e in range(width):
         for k in range(jl // LANES):
             block = wide_ref.at[k][pl.ds(e, seqs, stride=width), :]
-            rt_ref[e * seqs : (e + 1) * seqs, k * LANES : (k + 1) * LANES] = block.astype(BF16)
-    for n in range(0, width * seqs, LANES):
-        right_ref[:, n : n + LANES] = rt_ref[n : n + LANES, :].astype(F32).T.astype(BF16)
+            rt_ref[k, e * seqs : (e + 1) * seqs, :] = block.astype(BF16)
+    for n in range(right_ref.shape[0]):
+        for k in range(jl // LANES):
+            block = rt_ref[k, n * LANES : (n + 1) * LANES, :].astype(F32).T
+            right_ref[n, k * LANES : (k + 1) * LANES, :] = block.astype(BF16)
 
 
 def u_kernel(
@@ -235,12 +251,17 @@
         dw_ref[...] = jnp.zeros_like(dw_ref)
 
     u_block(seqs, rt_ref, g_ref, u_ref)
-    size, width, z = u_ref.shape[0], w_ref.shape[0], g_ref.shape[2]
-    start = pl.multiple_of(pl.program_id(0) * size, size)
-    dl_ref[pl.ds(start, size), :width] = dot(u_ref[...], w_ref[...], 1, 1)
+    count, size, z = u_ref.shape
+    width = w_ref.shape[0]
+    rows = min(size, 256)
+    for m in range(0, size, rows):
+        start = pl.multiple_of(pl.program_id(0) * size + m, rows)
+        block = lanes(u_ref[e, m : m + rows, :] for e in range(count))
+        dl_ref[pl.ds(start, rows), :width] = dot(block, w_ref[...], 1, 1)
     left_t = unpack(rows_ref[...], width, steps).T[:width].astype(BF16)
-    for n in range(0, u_ref.shape[1], 512):
-        dw_ref[:, n : n + 512] += dot(left_t, u_ref[:, n : n + 512])
+    for e in range(0, count, 4):
+        block = lanes(u_ref[e + k] for k in range(4))
+        dw_ref[:, e * z : (e + 4) * z] += dot(left_t, block)
 
     @pl.when(last())
     def _():
@@ -338,16 +359,22 @@
     shape = jax.ShapeDtypeStruct
     x_t = x.transpose(0, 2, 1)
 
-    left_send, right_send = call(
-        functools.partial(project_kernel, rows, cols),
+    (left_send,) = call(
+        functools.partial(left_kernel, rows, cols),
         (1,),
         [whole(x_t.shape), whole(split.shape)],
-        [
-            (whole((seqs, part, LANES)), shape((seqs, part, LANES), BF16)),
-            (whole((seqs, width, jl)), shape((seqs, width, jl), BF16)),
-        ],
+        [(whole((seqs, part, LANES)), shape((seqs, part, LANES), BF16))],
         [],
-        2 * length * depth * depth,
+        2 * length * depth * width,
+        (x_t, split),
+    )
+    (right_send,) = call(
+        functools.partial(project_right_kernel, rows, cols),
+        (1,),
+        [whole(x_t.shape), whole(split.shape)],
+        [(whole((seqs, width, jl)), shape((seqs, width, jl), BF16))],
+        [],
+        2 * length * depth * width,
         (x_t, split),
     )
     left_all = lax.all_to_all(left_send, AXES, 0, 0, tiled=True)
@@ -363,10 +390,16 @@
         (whole((width, width * z)), pltpu.HBM((width, width * z), BF16)),
     ]
     wides = [pltpu.VMEM((part * seqs, LANES), F32), pltpu.VMEM(couple.shape, F32)]
-    t_shape = (il // step, width * seqs, step * z)
+    t_shape = (il // step, step, width * seqs, z)
     depth = min(DEPTH, t_shape[0])
     any_spec = pl.BlockSpec(memory_space=pl.ANY)
     slots = [pltpu.VMEM((depth, *t_shape[1:]), BF16), pltpu.SemaphoreType.DMA((depth,))]
+    half = step // 2
+    half_depth = min(DEPTH + 1, il // half)
+    half_slots = [
+        pltpu.VMEM((half_depth, half, *t_shape[2:]), BF16),
+        pltpu.SemaphoreType.DMA((half_depth,)),
+    ]
     stored = 2 * math.prod(t_shape) <= STORED_BYTES
     if stored:
         left_rows, weight, t_all = call(
@@ -376,7 +409,8 @@
             arranged + [(any_spec, shape(t_shape, BF16))],
             wides + slots,
             small,
-            (left_all, couple),
+            (left_all, in_hbm(couple)),
+            limit=SMALL_BYTES,
         )
         right_all, t_all = lax.optimization_barrier((right_all, t_all))
     else:
@@ -391,7 +425,7 @@
         )
     share = width * width // seqs
     left_rows, weight = in_hbm(left_rows), in_hbm(weight)
-    right_shape = (jl, width * seqs)
+    right_shape = (width * seqs // LANES, jl, LANES)
     send_one, right = call(
         functools.partial(u_kernel, seqs, steps),
         grid,
@@ -404,10 +438,10 @@
             (whole(right_shape), pltpu.HBM(right_shape, BF16)),
         ],
         [
-            pltpu.VMEM((step * seqs, width * z), BF16),
+            pltpu.VMEM((width, step * seqs, z), BF16),
             pltpu.VMEM((il * seqs, LANES), F32),
             pltpu.VMEM((width, width * z), F32),
-            pltpu.VMEM((width * seqs, jl), BF16),
+            pltpu.VMEM((jl // LANES, width * seqs, LANES), BF16),
             pltpu.VMEM((jl // LANES, width * seqs, LANES), F32),
         ],
         unit + 2 * small,
@@ -429,12 +463,12 @@
         )
         (pair,) = call(
             pair_kernel,
-            grid,
+            (il // half,),
             [whole(right.shape), whole(bias_row.shape), any_spec],
-            [(cot_spec, shape(cot.shape, BF16))],
-            slots,
+            [(pl.BlockSpec((half, jl, z), lambda i: (i, 0, 0)), shape(cot.shape, BF16))],
+            half_slots,
             unit,
-            (right, bias_row, t_all),
+            (right, bias_row, t_all.reshape(il // half, half, *t_shape[2:])),
         )
     else:
         pair, right_back = call(
@@ -442,7 +476,7 @@
             grid,
             [rows_spec, whole(weight.shape), whole(right.shape), cot_spec, whole(bias_row.shape)],
             [(cot_spec, shape(cot.shape, BF16)), right_out],
-            [pltpu.VMEM((width * seqs, step * z), BF16), acc],
+            [pltpu.VMEM(t_shape[1:], BF16), acc],
             2 * unit + small,
             (left_rows, weight, right, cot, bias_row),
         )

time: 120 us -> 118 us (0.983)
  blocking collectives: 17.5 us -> 0 us
  waiting for transfers between devices: 4.38 us -> 13.5 us
  starting transfers between devices: 14.2 us -> 21.1 us
    all_to_all x1 -> x0, blocking collectives: 17.5 us -> none  [on_device(): left_all = lax.all_to_all(left_send, AXES, 0, 0, tiled=True)]
    all_to_all x0 -> x1, waiting for transfers between devices: none -> 8.33 us  [on_device(): left_all = lax.all_to_all(left_send, AXES, 0, 0, tiled=True)]
    all_to_all x0 -> x1, starting transfers between devices: none -> 7.08 us  [on_device(): left_all = lax.all_to_all(left_send, AXES, 0, 0, tiled=True)]
    pallas_call x7 -> x8, Pallas kernels: 83.1 us -> 82.2 us  [call(): pl.pallas_call(kernel, grid_spec=pltpu.PrefetchScalarGridSpec(num_scalar_...]
  transfers between devices with their start and end apart: 3 -> 4, of which waited for: 1 -> 3; matrix products, arithmetic and copies ran while one was open for 0% -> 0% of each run, Pallas kernels for 41% -> 42%
where the time goes in v3:
time: 118 us
  Pallas kernels  82.2 us (70%)
  starting transfers between devices  21.1 us (18%)
  waiting for transfers between devices  13.5 us (11%)
    pallas_call x8, Pallas kernels, call(): pl.pallas_call(kernel, grid_spec=pltpu.PrefetchScalarGridSpec(num_scalar_...  82.2 us
    all_to_all x1, waiting for transfers between devices, on_device(): left_all = lax.all_to_all(left_send, AXES, 0, 0, tiled=True)  8.33 us
    all_to_all x1, starting transfers between devices, on_device(): left_all = lax.all_to_all(left_send, AXES, 0, 0, tiled=True)  7.08 us
    all_to_all x1, starting transfers between devices, on_device(): got_two = lax.all_to_all(send_two, AXES, 0, 0, tiled=True)  5.85 us
    all_to_all x1, starting transfers between devices, on_device(): got_one = lax.all_to_all(send_one, AXES, 0, 0, tiled=True)  5.59 us
    all_to_all x1, waiting for transfers between devices, on_device(): got_two = lax.all_to_all(send_two, AXES, 0, 0, tiled=True)  4.87 us
    all_to_all x1, starting transfers between devices, on_device(): right_all = lax.all_to_all(right_send, AXES, 0, 0, tiled=True)  2.57 us
  transfers between devices with their start and end apart: 4, of which 3 were waited for; matrix products, arithmetic and copies ran while one was open for 0% of the time, Pallas kernels for 42%

profile of v3, /device:TPU:1, one launch (start us, length us, event | category | flops | bytes accessed | tf_op | source)
XLA Modules:
  0.0 117.5 jit_solution(12206235317800982121)
XLA Ops:
  0.6 2.0 %shard_map.76 = bf16[32,32,128]{2,1,0:T(8,128)(2,1)} custom-call(bf16[1,64,1024]{2,1,0:T(8,128)(2,1)} %bitcast.4, bf16[64,64]{1,0:T(8,128)(2,1)} %w_ref.5), custom_call_target="tpu_custom_call" | custom-call | flops 4194304 | bytes 401408 | tf_op jit(solution)/shard_map/pallas_call | solution.py:41
  2.7 7.1 %all-to-all-start = ((bf16[32,32,128]{2,1,0:T(8,128)(2,1)}), bf16[32,32,128]{2,1,0:T(8,128)(2,1)S(1)}, u32[]{:S(2)}, u32[]{:S(2)}) async-start(bf16[32,32,128]{2,1,0:T(8,128)(2,1)} %shard_map.76), calls=%async_computation | async-start | bytes 524288 | tf_op jit(solution)/shard_map/all_to_all | solution.py:380
  9.7 2.0 %shard_map.78 = bf16[32,32,256]{2,1,0:T(8,128)(2,1)} custom-call(bf16[1,64,1024]{2,1,0:T(8,128)(2,1)} %bitcast.5, bf16[64,64]{1,0:T(8,128)(2,1)} %w_ref.5), custom_call_target="tpu_custom_call" | custom-call | flops 4194304 | bytes 663552 | tf_op jit(solution)/shard_map/pallas_call | solution.py:41
  11.7 8.3 %all-to-all-done.left_ref = bf16[32,32,128]{2,1,0:T(8,128)(2,1)S(1)} async-done(((bf16[32,32,128]{2,1,0:T(8,128)(2,1)}), bf16[32,32,128]{2,1,0:T(8,128)(2,1)S(1)}, u32[]{:S(2)}, u32[]{:S(2)}) %all-to-all-start) | async-done | bytes 262176 | tf_op jit(solution)/shard_map/all_to_all | solution.py:380
  20.1 2.6 %all-to-all-start.1 = ((bf16[32,32,256]{2,1,0:T(8,128)(2,1)}), bf16[32,32,256]{2,1,0:T(8,128)(2,1)S(1)}, u32[]{:S(2)}, u32[]{:S(2)}) async-start(bf16[32,32,256]{2,1,0:T(8,128)(2,1)} %shard_map.78), calls=%async_computation.1 | async-start | bytes 1048576 | tf_op jit(solution)/shard_map/all_to_all | solution.py:381
  22.6 15.0 %shard_map.77 = (bf16[1024,128]{1,0:T(8,128)(2,1)}, bf16[32,4096]{1,0:T(8,128)(2,1)}, bf16[8,16,1024,128]{3,2,1,0:T(8,128)(2,1)}) custom-call(bf16[32,32,128]{2,1,0:T(8,128)(2,1)S(1)} %all-to-all-done.left_ref, bf16[1024,128]{1,0:T(8,128)(2,1)} %couple_ref.1), custom_call_target="tpu_custom_call" | custom-call | flops 1073741824 | bytes 34603008 | tf_op jit(solution)/shard_map/pallas_call | solution.py:41
  37.6 0.3 all-to-all-done.1.all_ref
  37.9 28.4 %shard_map.79 = (bf16[32,64,128]{2,1,0:T(8,128)(2,1)}, bf16[8,256,128]{2,1,0:T(8,128)(2,1)}) custom-call(bf16[1024,128]{1,0:T(8,128)(2,1)} %get-tuple-element.12.rows_ref, bf16[32,32,256]{2,1,0:T(8,128)(2,1)S(1)} %all-to-all-done.1.all_ref, bf16[128,256,128]{2,1,0:T(8,128)(2,1)} %g_ref.3, bf16[32,4096]{1,0:T(8,128)(2,1)} %get-tuple-element.15.w_ref), custom_call_target="tpu_custom_call" | custom-call | flops 10737418240 | bytes 10485760 | tf_op jit(solution)/shard_map/pallas_call | solution.py:41
  66.4 5.6 %all-to-all-start.2 = ((bf16[32,64,128]{2,1,0:T(8,128)(2,1)}), bf16[32,64,128]{2,1,0:T(8,128)(2,1)S(1)}, u32[]{:S(2)}, u32[]{:S(2)}) async-start(bf16[32,64,128]{2,1,0:T(8,128)(2,1)} %get-tuple-element.18), calls=%async_computation.2 | async-start | bytes 1048576 | tf_op jit(solution)/shard_map/all_to_all | solution.py:451
  72.0 16.5 %shard_map.81._ = bf16[32,32,384]{2,1,0:T(8,128)(2,1)} custom-call(bf16[8,16,1024,128]{3,2,1,0:T(8,128)(2,1)} %get-tuple-element.17.t_ref, bf16[128,256,128]{2,1,0:T(8,128)(2,1)} %g_ref.3), custom_call_target="tpu_custom_call" | custom-call | flops 8589934592 | bytes 42729472 | tf_op jit(solution)/shard_map/pallas_call | solution.py:41
  88.5 0.0 all-to-all-done.2.parts_ref.left_ref
  88.5 0.8 shard_map.82
  89.3 5.8 %all-to-all-start.3 = ((bf16[32,32,384]{2,1,0:T(8,128)(2,1)}), bf16[32,32,384]{2,1,0:T(8,128)(2,1)S(1)}, u32[]{:S(2)}, u32[]{:S(2)}) async-start(bf16[32,32,384]{2,1,0:T(8,128)(2,1)} %shard_map.82), calls=%async_computation.3 | async-start | bytes 1572864 | tf_op jit(solution)/shard_map/all_to_all | solution.py:502
  95.2 0.0 copy-start
  95.2 0.0 copy-start.1
  95.2 15.9 %shard_map.80 = bf16[128,256,128]{2,1,0:T(8,128)(2,1)} custom-call(bf16[8,256,128]{2,1,0:T(8,128)(2,1)} %get-tuple-element.16.r_ref, bf16[1,128]{1,0:T(2,128)(2,1)} %bitcast.8, bf16[16,8,1024,128]{3,2,1,0:T(8,128)(2,1)} %bitcast.7), custom_call_target="tpu_custom_call" | custom-call | flops 8589934592 | bytes 42467584 | tf_op jit(solution)/shard_map/pallas_call | solution.py:41
  111.1 4.9 %all-to-all-done.3.right_ref = bf16[32,32,384]{2,1,0:T(8,128)(2,1)S(1)} async-done(((bf16[32,32,384]{2,1,0:T(8,128)(2,1)}), bf16[32,32,384]{2,1,0:T(8,128)(2,1)S(1)}, u32[]{:S(2)}, u32[]{:S(2)}) %all-to-all-start.3) | async-done | bytes 786464 | tf_op jit(solution)/shard_map/all_to_all | solution.py:502
  116.0 0.0 copy-done
  116.0 0.0 copy-done.1
  116.0 1.6 %shard_map.83 = (bf16[1,64,1024]{2,1,0:T(8,128)(2,1)}, f32[1024,128]{1,0:T(8,128)}) custom-call(bf16[32,64,128]{2,1,0:T(8,128)(2,1)S(1)} %all-to-all-done.2.parts_ref.left_ref, bf16[32,32,384]{2,1,0:T(8,128)(2,1)S(1)} %all-to-all-done.3.right_ref, bf16[1,64,1024]{2,1,0:T(8,128)(2,1)S(1)} %bitcast.6, bf16[64,64]{1,0:T(8,128)(2,1)S(1)} %copy-done.1), custom_call_target="tpu_custom_call" | custom-call | flops 18432 | bytes 2105344 | tf_op jit(solution)/shard_map/pallas_call | solution.py:41
Async XLA Ops:
  2.7 17.4 %all-to-all-start = ((bf16[32,32,128]{2,1,0:T(8,128)(2,1)}), bf16[32,32,128]{2,1,0:T(8,128)(2,1)S(1)}, u32[]{:S(2)}, u32[]{:S(2)}) async-start(bf16[32,32,128]{2,1,0:T(8,128)(2,1)} %shard_map.76), calls=%async_computation | async-start | bytes 524288 | tf_op jit(solution)/shard_map/all_to_all | solution.py:380
  20.1 17.8 %all-to-all-start.1 = ((bf16[32,32,256]{2,1,0:T(8,128)(2,1)}), bf16[32,32,256]{2,1,0:T(8,128)(2,1)S(1)}, u32[]{:S(2)}, u32[]{:S(2)}) async-start(bf16[32,32,256]{2,1,0:T(8,128)(2,1)} %shard_map.78), calls=%async_computation.1 | async-start | bytes 1048576 | tf_op jit(solution)/shard_map/all_to_all | solution.py:381
  66.4 22.1 %all-to-all-start.2 = ((bf16[32,64,128]{2,1,0:T(8,128)(2,1)}), bf16[32,64,128]{2,1,0:T(8,128)(2,1)S(1)}, u32[]{:S(2)}, u32[]{:S(2)}) async-start(bf16[32,64,128]{2,1,0:T(8,128)(2,1)} %get-tuple-element.18), calls=%async_computation.2 | async-start | bytes 1048576 | tf_op jit(solution)/shard_map/all_to_all | solution.py:451
  89.3 26.6 %all-to-all-start.3 = ((bf16[32,32,384]{2,1,0:T(8,128)(2,1)}), bf16[32,32,384]{2,1,0:T(8,128)(2,1)S(1)}, u32[]{:S(2)}, u32[]{:S(2)}) async-start(bf16[32,32,384]{2,1,0:T(8,128)(2,1)} %shard_map.82), calls=%async_computation.3 | async-start | bytes 1572864 | tf_op jit(solution)/shard_map/all_to_all | solution.py:502
  95.2 20.8 %copy-start = (bf16[1,1024,64]{1,2,0:T(8,128)(2,1)S(1)}, bf16[1,1024,64]{1,2,0:T(8,128)(2,1)}, u32[]{:S(2)}) copy-start(bf16[1,1024,64]{1,2,0:T(8,128)(2,1)} %param.5) | copy-start | bytes 393220
  95.2 20.8 %copy-start.1 = (bf16[64,64]{1,0:T(8,128)(2,1)S(1)}, bf16[64,64]{1,0:T(8,128)(2,1)}, u32[]{:S(2)}) copy-start(bf16[64,64]{1,0:T(8,128)(2,1)} %w_ref.5) | copy-start | bytes 24580
